TPU v7x, 32 devices: a whole 2x2x4 slice. The times are simulated.
32 devices in a mesh: wide: 8 (over z, x), narrow: 4 (over y, core).
Axes of the slice: x: 2, y: 2, z: 4, core: 2. Of those that a mesh axis runs over, the one named last changes fastest.
Arguments:
- tokens: bfloat16 [4096, 2048], P('wide', 'narrow'), may hold values from -6 to 6
- cotangent: bfloat16 [4096, 2048], P('wide', 'narrow'), may hold values from -6 to 6
- block_ids: int32 [8, 512], P('wide'), may hold values from 0 to 2, never falling along the last dimension, each value on 1 to 256 neighbouring positions
- routes: int32 [4096, 8], P('wide'), may hold values from 0 to 15, all different within a row; in each aligned block of 512 rows (0 to 511, 512 to 1023, ...) at most 272 rows name the same one
- norm_attn: bfloat16 [2048], P('narrow'), may hold values from 0.5 to 1.5
- w_query: bfloat16 [2048, 2048], P('wide', 'narrow'), may hold values from -0.125 to 0.125
- w_key: bfloat16 [2048, 2048], P('wide', 'narrow'), may hold values from -0.125 to 0.125
- w_value: bfloat16 [2048, 2048], P('wide', 'narrow'), may hold values from -0.125 to 0.125
- norm_query: bfloat16 [2048], P('narrow'), may hold values from 0.5 to 1.5
- norm_key: bfloat16 [2048], P('narrow'), may hold values from 0.5 to 1.5
- w_out: bfloat16 [2048, 2048], P('wide', 'narrow'), may hold values from -1 to 1
- norm_ffn: bfloat16 [2048], P('narrow'), may hold values from 0.5 to 1.5
- w_router: bfloat16 [2048, 16], replicated, may hold values from -0.0625 to 0.0625
- w_gate: bfloat16 [2048, 16, 1024], P('wide', None, 'narrow'), may hold values from -0.125 to 0.125
- w_up: bfloat16 [2048, 16, 1024], P('wide', None, 'narrow'), may hold values from -0.125 to 0.125
- w_down: bfloat16 [2048, 16, 1024], P('wide', None, 'narrow'), may hold values from -1.5 to 1.5
Outputs:
- block_out: bfloat16 [4096, 2048], P('wide', 'narrow')
- grad_tokens: float32 [4096, 2048], P('wide', 'narrow')
- grad_norm_attn: float32 [2048], P('narrow')
- grad_query: float32 [2048, 2048], P('wide', 'narrow')
- grad_key: float32 [2048, 2048], P('wide', 'narrow')
- grad_value: float32 [2048, 2048], P('wide', 'narrow')
- grad_norm_query: float32 [2048], P('narrow')
- grad_norm_key: float32 [2048], P('narrow')
- grad_out: float32 [2048, 2048], P('wide', 'narrow')
- grad_norm_ffn: float32 [2048], P('narrow')
- grad_router: float32 [2048, 16], replicated
- grad_gate: float32 [2048, 16, 1024], P('wide', None, 'narrow')
- grad_up: float32 [2048, 16, 1024], P('wide', None, 'narrow')
- grad_down: float32 [2048, 16, 1024], P('wide', None, 'narrow')
Inputs may be any that keep to these rules, and one draw needn't show every extreme that they name: `block_ids`: block numbers never fall along a sequence; each block has 1 to 256 tokens and some block exactly 256. `routes`: each row names 8 different experts; among the tokens of one sequence no expert is named more than 272 times, a bound that some block reaches.
All inputs are finite; a program needn't handle non-finite values.
Results may differ from a plain program's by a relative error of at most 0.025.
Values may be sent and summed in bfloat16 or wider, within the bound.
No kernel may reach another device: no remote copies, remote signals or barrier semaphores. Data moves between devices by JAX's collectives and lax.ppermute only.
A program may use at most 384 MiB of HBM per device.

v0:
```python
import jax
import jax.numpy as jnp
from jax import lax
from jax.sharding import PartitionSpec as P

HD = 128
EXPERTS = 16
TOP = 8
CAP = 272
EPS = 1e-05
query_rows = 512


def rms_scale(values, scales):
    return values * lax.rsqrt(jnp.mean(values * values, axis=-1, keepdims=True) + EPS) * scales


def rope_tables(length, head_dim):
    exponent = jnp.arange(0, head_dim, 2, dtype=jnp.float32) / head_dim
    angles = jnp.arange(length, dtype=jnp.float32)[:, None] * (10000.0 ** (-exponent))[None, :]
    angles = jnp.concatenate([angles, angles], axis=-1)
    return (jnp.cos(angles)[:, None, :], jnp.sin(angles)[:, None, :])


def rotate_half(values, cosines, sine_table):
    middle = values.shape[-1] // 2
    turned = jnp.concatenate([-values[..., middle:], values[..., :middle]], axis=-1)
    return values * cosines + turned * sine_table


def slot_tables(routes, experts, capacity):
    token_count, top_count = routes.shape
    flat_routes = routes.reshape(-1)
    onehot = (flat_routes[:, None] == jnp.arange(experts, dtype=jnp.int32)[None, :]).astype(
        jnp.int32
    )
    earlier = jnp.cumsum(onehot, axis=0) - onehot
    within = jnp.sum(earlier * onehot, axis=1)
    destination = flat_routes * capacity + within
    pair_ids = jnp.arange(token_count * top_count, dtype=jnp.int32)
    owners = (
        jnp.full((experts * capacity,), token_count * top_count, jnp.int32)
        .at[destination]
        .set(pair_ids)
    )
    return (destination.reshape(token_count, top_count), owners)


def swiglu(gate_in, up_in):
    return jax.nn.silu(gate_in) * up_in


def per_device(
    tokens,
    cotangent,
    block_ids,
    routes,
    norm_attn,
    w_query,
    w_key,
    w_value,
    norm_query,
    norm_key,
    w_out,
    norm_ffn,
    w_router,
    w_gate,
    w_up,
    w_down,
):
    lane_index = lax.axis_index("narrow")
    rows_full, cot_full, gain_attn, gain_ffn = (
        lax.all_gather(tokens, "narrow", axis=1, tiled=True),
        lax.all_gather(cotangent, "narrow", axis=1, tiled=True),
        lax.all_gather(norm_attn, "narrow", axis=0, tiled=True),
        lax.all_gather(norm_ffn, "narrow", axis=0, tiled=True),
    )
    length, model_width = rows_full.shape
    head_cols = w_query.shape[1]
    heads_here = head_cols // HD
    score_scale = HD ** (-0.5)
    rows_float = rows_full.astype(jnp.float32)
    cot_float = cot_full.astype(jnp.float32)
    attn_gain = gain_attn.astype(jnp.float32)
    ffn_gain = gain_ffn.astype(jnp.float32)
    normed = rms_scale(rows_float, attn_gain).astype(jnp.bfloat16)
    query_full, key_full, value_full = (
        lax.all_gather(w_query, "wide", axis=0, tiled=True),
        lax.all_gather(w_key, "wide", axis=0, tiled=True),
        lax.all_gather(w_value, "wide", axis=0, tiled=True),
    )
    query_raw = jnp.dot(normed, query_full, preferred_element_type=jnp.float32)
    key_raw = jnp.dot(normed, key_full, preferred_element_type=jnp.float32)
    value_raw = jnp.dot(normed, value_full, preferred_element_type=jnp.float32)
    square_query, square_key = lax.psum(
        (jnp.sum(query_raw * query_raw, axis=1), jnp.sum(key_raw * key_raw, axis=1)), "narrow"
    )
    query_scale = lax.rsqrt(square_query / model_width + EPS)[:, None]
    key_scale = lax.rsqrt(square_key / model_width + EPS)[:, None]
    query_gain = norm_query.astype(jnp.float32)
    key_gain = norm_key.astype(jnp.float32)
    cosines, sine_table = rope_tables(length, HD)
    query_normed = query_raw * query_scale * query_gain
    key_normed = key_raw * key_scale * key_gain

    def rotate_both(query_in, key_in):
        return (
            rotate_half(query_in.reshape(length, heads_here, HD), cosines, sine_table),
            rotate_half(key_in.reshape(length, heads_here, HD), cosines, sine_table),
        )

    (query_rot, key_rot), rotate_pull = jax.vjp(rotate_both, query_normed, key_normed)
    query_bf = query_rot.astype(jnp.bfloat16)
    key_bf = key_rot.astype(jnp.bfloat16)
    value_bf = value_raw.astype(jnp.bfloat16).reshape(length, heads_here, HD)
    seq_blocks = block_ids[0]
    step_rows = min(query_rows, length)

    def block_scores(offset):
        scores = (
            jnp.einsum("qhd,khd->hqk", query_bf, key_bf, preferred_element_type=jnp.float32)
            * score_scale
        )
        allowed = seq_blocks[None, :] <= seq_blocks[offset : offset + step_rows, None]
        return jnp.where(allowed[None], scores, -1e30)

    offset = 0
    scores = block_scores(offset)
    highest = jnp.max(scores, axis=-1, keepdims=True)
    shifted = jnp.exp(scores - highest)
    totals = jnp.sum(shifted, axis=-1, keepdims=True)
    attn_probs = (shifted / totals).astype(jnp.bfloat16)
    attended_parts = jnp.einsum(
        "hqk,khd->qhd", attn_probs, value_bf, preferred_element_type=jnp.float32
    ).astype(jnp.bfloat16)
    total_parts = highest + jnp.log(totals)
    attended = attended_parts.reshape(length, head_cols)
    out_full = lax.all_gather(w_out, "wide", axis=0, tiled=True)
    out_partial = jnp.einsum("td,cd->tc", attended, out_full, preferred_element_type=jnp.float32)
    residual = rows_float + lax.psum(out_partial, "narrow")
    ffn_in = rms_scale(residual, ffn_gain).astype(jnp.bfloat16)
    logits = jnp.dot(ffn_in, w_router, preferred_element_type=jnp.float32)

    def route_gates(logit_values):
        return jnp.take_along_axis(jax.nn.softmax(logit_values, axis=-1), routes, axis=1)

    gate_values, gate_pull = jax.vjp(route_gates, logits)
    destination, owners = slot_tables(routes, EXPERTS, CAP)
    slot_tokens = owners // TOP
    slot_gates = jnp.concatenate([gate_values.reshape(-1), jnp.zeros((1,), jnp.float32)], axis=0)[
        owners
    ]
    padded_in = jnp.concatenate([ffn_in, jnp.zeros((1, model_width), jnp.bfloat16)], axis=0)
    expert_rows = padded_in[slot_tokens].reshape(EXPERTS, CAP, model_width)
    padded_cot = jnp.concatenate([cot_float, jnp.zeros((1, model_width), jnp.float32)], axis=0)
    slot_cot = padded_cot[slot_tokens]
    gate_full, up_full = (
        lax.all_gather(w_gate, "wide", axis=0, tiled=True),
        lax.all_gather(w_up, "wide", axis=0, tiled=True),
    )
    gate_pre = jnp.einsum(
        "ecd,def->ecf", expert_rows, gate_full, preferred_element_type=jnp.float32
    )
    up_pre = jnp.einsum("ecd,def->ecf", expert_rows, up_full, preferred_element_type=jnp.float32)
    hidden_float, swiglu_pull = jax.vjp(swiglu, gate_pre, up_pre)
    hidden_bf = hidden_float.astype(jnp.bfloat16)
    down_full = lax.all_gather(w_down, "wide", axis=0, tiled=True)
    expert_out = jnp.einsum(
        "ecf,def->ecd", hidden_bf, down_full, preferred_element_type=jnp.float32
    ).reshape(EXPERTS * CAP, model_width)
    moe_partial = (
        jnp.zeros((length + 1, model_width), jnp.float32)
        .at[slot_tokens]
        .add(slot_gates[:, None] * expert_out)[:length]
    )
    slot_dots = jnp.concatenate(
        [jnp.sum(expert_out * slot_cot, axis=1), jnp.zeros((1,), jnp.float32)], axis=0
    )
    dots_partial = slot_dots[destination]
    expert_cot = (
        (slot_gates[:, None] * slot_cot).astype(jnp.bfloat16).reshape(EXPERTS, CAP, model_width)
    )
    hidden_grad = jnp.einsum(
        "ecd,def->ecf", expert_cot, down_full, preferred_element_type=jnp.float32
    )
    gate_grad, up_grad = swiglu_pull(hidden_grad)
    gate_grad_bf = gate_grad.astype(jnp.bfloat16)
    up_grad_bf = up_grad.astype(jnp.bfloat16)
    rows_grad = jnp.einsum(
        "ecf,def->ecd", gate_grad_bf, gate_full, preferred_element_type=jnp.float32
    ) + jnp.einsum("ecf,def->ecd", up_grad_bf, up_full, preferred_element_type=jnp.float32)
    input_partial = (
        jnp.zeros((length + 1, model_width), jnp.float32)
        .at[slot_tokens]
        .add(rows_grad.reshape(EXPERTS * CAP, model_width))[:length]
    )
    pair_dots, input_sum, moe_sum = (
        lax.psum(dots_partial.astype(jnp.bfloat16), "narrow").astype(jnp.float32),
        lax.psum(input_partial.astype(jnp.bfloat16), "narrow").astype(jnp.float32),
        lax.psum(moe_partial.astype(jnp.bfloat16), "narrow").astype(jnp.float32),
    )
    block_rows = residual + moe_sum
    block_out = lax.dynamic_slice_in_dim(block_rows, lane_index * head_cols, head_cols, 1).astype(
        jnp.bfloat16
    )
    logit_grad = gate_pull(pair_dots)[0].astype(jnp.bfloat16)
    ffn_grad = input_sum + jnp.einsum(
        "te,de->td", logit_grad, w_router, preferred_element_type=jnp.float32
    )
    router_grad = jnp.einsum("td,te->de", ffn_in, logit_grad, preferred_element_type=jnp.float32)
    _, ffn_norm_pull = jax.vjp(rms_scale, residual, ffn_gain)
    residual_norm_grad, ffn_gain_grad = ffn_norm_pull(ffn_grad)
    residual_grad = cot_float + residual_norm_grad
    out_cot = residual_grad.astype(jnp.bfloat16)
    attended_grad = (
        jnp.einsum("tc,cd->td", out_cot, out_full, preferred_element_type=jnp.float32)
        .astype(jnp.bfloat16)
        .reshape(length, heads_here, HD)
    )
    offset = 0
    scores = block_scores(offset)
    attn_probs = jnp.exp(scores - total_parts)
    prob_grad = jnp.einsum(
        "qhd,khd->hqk", attended_grad, value_bf, preferred_element_type=jnp.float32
    )
    centre = jnp.sum(attn_probs * prob_grad, axis=-1, keepdims=True)
    score_grad = (attn_probs * (prob_grad - centre)).astype(jnp.bfloat16)
    query_grad_parts = (
        jnp.einsum("hqk,khd->qhd", score_grad, key_bf, preferred_element_type=jnp.float32)
        * score_scale
    )
    key_grad = (
        jnp.einsum("hqk,qhd->khd", score_grad, query_bf, preferred_element_type=jnp.float32)
        * score_scale
    )
    value_grad = jnp.einsum(
        "hqk,qhd->khd",
        attn_probs.astype(jnp.bfloat16),
        attended_grad,
        preferred_element_type=jnp.float32,
    )
    query_normed_grad, key_normed_grad = rotate_pull((query_grad_parts, key_grad))
    dot_query, dot_key = lax.psum(
        (
            jnp.sum(query_gain * query_normed_grad * query_raw, axis=1),
            jnp.sum(key_gain * key_normed_grad * key_raw, axis=1),
        ),
        "narrow",
    )
    query_pre_grad = (
        query_scale * query_gain * query_normed_grad
        - query_raw * query_scale**3 * dot_query[:, None] / model_width
    )
    key_pre_grad = (
        key_scale * key_gain * key_normed_grad
        - key_raw * key_scale**3 * dot_key[:, None] / model_width
    )
    query_gain_grad = jnp.sum(query_normed_grad * query_raw * query_scale, axis=0)
    key_gain_grad = jnp.sum(key_normed_grad * key_raw * key_scale, axis=0)
    query_grad_bf = query_pre_grad.astype(jnp.bfloat16)
    key_grad_bf = key_pre_grad.astype(jnp.bfloat16)
    value_grad_bf = value_grad.reshape(length, head_cols).astype(jnp.bfloat16)
    normed_partial = jnp.einsum(
        "tc,dc->td", query_grad_bf, query_full, preferred_element_type=jnp.float32
    )
    normed_partial = normed_partial + jnp.einsum(
        "tc,dc->td", key_grad_bf, key_full, preferred_element_type=jnp.float32
    )
    normed_partial = normed_partial + jnp.einsum(
        "tc,dc->td", value_grad_bf, value_full, preferred_element_type=jnp.float32
    )
    normed_grad = lax.psum(normed_partial.astype(jnp.bfloat16), "narrow").astype(jnp.float32)
    _, attn_norm_pull = jax.vjp(rms_scale, rows_float, attn_gain)
    rows_norm_grad, attn_gain_grad = attn_norm_pull(normed_grad)
    grad_tokens = lax.dynamic_slice_in_dim(
        residual_grad + rows_norm_grad, lane_index * head_cols, head_cols, 1
    )
    small_terms = (
        router_grad,
        lax.dynamic_slice_in_dim(attn_gain_grad, lane_index * head_cols, head_cols, 0),
        lax.dynamic_slice_in_dim(ffn_gain_grad, lane_index * head_cols, head_cols, 0),
        query_gain_grad,
        key_gain_grad,
    )
    grad_router, grad_norm_attn, grad_norm_ffn, grad_norm_query, grad_norm_key = (
        lax.psum(small_terms[0].astype(jnp.bfloat16), "wide").astype(jnp.float32),
        lax.psum(small_terms[1].astype(jnp.bfloat16), "wide").astype(jnp.float32),
        lax.psum(small_terms[2].astype(jnp.bfloat16), "wide").astype(jnp.float32),
        lax.psum(small_terms[3].astype(jnp.bfloat16), "wide").astype(jnp.float32),
        lax.psum(small_terms[4].astype(jnp.bfloat16), "wide").astype(jnp.float32),
    )
    query_term = jnp.einsum("tc,tf->cf", normed, query_grad_bf, preferred_element_type=jnp.float32)
    key_term = jnp.einsum("tc,tf->cf", normed, key_grad_bf, preferred_element_type=jnp.float32)
    value_term = jnp.einsum("tc,tf->cf", normed, value_grad_bf, preferred_element_type=jnp.float32)
    out_term = jnp.einsum("tc,tf->cf", out_cot, attended, preferred_element_type=jnp.float32)
    gate_term = jnp.einsum(
        "ecd,ecf->def", expert_rows, gate_grad_bf, preferred_element_type=jnp.float32
    )
    up_term = jnp.einsum(
        "ecd,ecf->def", expert_rows, up_grad_bf, preferred_element_type=jnp.float32
    )
    down_term = jnp.einsum(
        "ecd,ecf->def", expert_cot, hidden_bf, preferred_element_type=jnp.float32
    )
    gate_term, up_term, down_term = (gate_term, up_term, down_term)
    grad_query, grad_key, grad_value, grad_out, grad_gate, grad_up, grad_down = (
        lax.psum_scatter(
            query_term.astype(jnp.bfloat16), "wide", scatter_dimension=0, tiled=True
        ).astype(jnp.float32),
        lax.psum_scatter(
            key_term.astype(jnp.bfloat16), "wide", scatter_dimension=0, tiled=True
        ).astype(jnp.float32),
        lax.psum_scatter(
            value_term.astype(jnp.bfloat16), "wide", scatter_dimension=0, tiled=True
        ).astype(jnp.float32),
        lax.psum_scatter(
            out_term.astype(jnp.bfloat16), "wide", scatter_dimension=0, tiled=True
        ).astype(jnp.float32),
        lax.psum_scatter(
            gate_term.astype(jnp.bfloat16), "wide", scatter_dimension=0, tiled=True
        ).astype(jnp.float32),
        lax.psum_scatter(
            up_term.astype(jnp.bfloat16), "wide", scatter_dimension=0, tiled=True
        ).astype(jnp.float32),
        lax.psum_scatter(
            down_term.astype(jnp.bfloat16), "wide", scatter_dimension=0, tiled=True
        ).astype(jnp.float32),
    )
    return (
        block_out,
        grad_tokens,
        grad_norm_attn,
        grad_query,
        grad_key,
        grad_value,
        grad_norm_query,
        grad_norm_key,
        grad_out,
        grad_norm_ffn,
        grad_router,
        grad_gate,
        grad_up,
        grad_down,
    )


def solution(mesh):
    placed = (
        P("wide", "narrow"),
        P("wide", "narrow"),
        P("wide", None),
        P("wide", None),
        P("narrow"),
        P("wide", "narrow"),
        P("wide", "narrow"),
        P("wide", "narrow"),
        P("narrow"),
        P("narrow"),
        P("wide", "narrow"),
        P("narrow"),
        P(),
        P("wide", None, "narrow"),
        P("wide", None, "narrow"),
        P("wide", None, "narrow"),
    )
    return jax.shard_map(
        per_device,
        mesh=mesh,
        in_specs=placed,
        out_specs=(
            P("wide", "narrow"),
            P("wide", "narrow"),
            P("narrow"),
            P("wide", "narrow"),
            P("wide", "narrow"),
            P("wide", "narrow"),
            P("narrow"),
            P("narrow"),
            P("wide", "narrow"),
            P("narrow"),
            P(),
            P("wide", None, "narrow"),
            P("wide", None, "narrow"),
            P("wide", None, "narrow"),
        ),
        check_vma=False,
    )
```

profile of v0, /device:TPU:0, one launch (start us, length us, event | category | flops | bytes accessed | tf_op | source)
XLA Modules:
  0.0 2680.0 jit_solution(7671028160317145200)
XLA Ops:
  11.9 6.1 all-gather
  22.9 12.0 all-gather.12.cloned.1.call-done
  37.0 49.3 %all-gather.16.cloned.1.call-done = bf16[2048,512]{1,0:T(8,128)(2,1)} async-done(((bf16[256,512]{1,0:T(8,128)(2,1)}), bf16[2048,512]{1,0:T(8,128)(2,1)}) %all-gather.16.cloned.1.call-update) | async-done | bytes 2097168 | tf_op jit(solution)/shard_map/all_gather | solution.py:88
  90.1 46.2 %all-gather.18.cloned.1.call-done = bf16[2048,512]{1,0:T(8,128)(2,1)} async-done(((bf16[256,512]{1,0:T(8,128)(2,1)}), bf16[2048,512]{1,0:T(8,128)(2,1)}) %all-gather.18.cloned.1.call-update) | async-done | bytes 2097168 | tf_op jit(solution)/shard_map/all_gather | solution.py:89
  140.2 5.6 all-reduce.7
  152.6 33.5 %all-gather.14.cloned.1.call-done = bf16[2048,512]{1,0:T(8,128)(2,1)} async-done(((bf16[256,512]{1,0:T(8,128)(2,1)}), bf16[2048,512]{1,0:T(8,128)(2,1)}) %all-gather.14.cloned.1.call-update) | async-done | bytes 2097168 | tf_op jit(solution)/shard_map/all_gather | solution.py:90
  191.0 44.9 %all-gather.20.cloned.1.call-done = bf16[2048,512]{1,0:T(8,128)(2,1)} async-done(((bf16[256,512]{1,0:T(8,128)(2,1)}), bf16[2048,512]{1,0:T(8,128)(2,1)}) %all-gather.20.cloned.1.call-update) | async-done | bytes 2097168 | tf_op jit(solution)/shard_map/all_gather | solution.py:138
  235.9 4.9 fusion.66
  252.9 5.2 all-gather.1
  266.1 15.5 scatter_custom_fusion
  287.1 34.3 %gather_fusion.2 = f32[4352,2048]{1,0:T(8,128)} fusion(f32[513,2048]{1,0:T(8,128)} %concatenate.34, s32[5120]{0:T(1024)S(1)} %pad_clamp_fusion), kind=kCustom, calls=%fused_computation.2 | custom fusion | bytes 71320576 | tf_op jit(solution)/shard_map/gather | solution.py:156
  322.0 24.9 all-reduce.15.cloned.1.call-done
  352.5 33.0 %gather_fusion.4 = f32[4096]{0:T(1024)S(1)} fusion(f32[512,16]{0,1:T(8,128)S(1)} %fusion.49, s32[4096]{0:T(1024)S(1)} %reshape.331), kind=kCustom, calls=%fused_computation.4 | custom fusion | bytes 65536 | tf_op jit(solution)/shard_map/jvp(jit(take_along_axis))/gather | solution.py:145
  386.2 22.8 gather_fusion
  411.4 17.2 gather_fusion.1
  429.2 147.9 %all-gather.22.cloned.1.call-done = bf16[2048,16,256]{2,0,1:T(8,128)(2,1)} async-done(((bf16[256,16,256]{2,0,1:T(8,128)(2,1)}), bf16[2048,16,256]{2,0,1:T(8,128)(2,1)}) %all-gather.22.cloned.1.call-update) | async-done | bytes 16777232 | tf_op jit(solution)/shard_map/all_gather | solution.py:158
  577.1 16.6 fusion.67
  593.7 211.7 %all-gather.24.cloned.1.call-done = bf16[2048,16,256]{2,0,1:T(8,128)(2,1)} async-done(((bf16[256,16,256]{2,0,1:T(8,128)(2,1)}), bf16[2048,16,256]{2,0,1:T(8,128)(2,1)}) %all-gather.24.cloned.1.call-update) | async-done | bytes 16777232 | tf_op jit(solution)/shard_map/all_gather | solution.py:159
  805.3 16.6 fusion.68
  821.9 211.5 %all-gather.26.cloned.1.call-done = bf16[2048,16,256]{2,0,1:T(8,128)(2,1)} async-done(((bf16[256,16,256]{2,0,1:T(8,128)(2,1)}), bf16[2048,16,256]{2,0,1:T(8,128)(2,1)}) %all-gather.26.cloned.1.call-update) | async-done | bytes 16777232 | tf_op jit(solution)/shard_map/all_gather | solution.py:167
  1033.4 34.2 %multiply_convert_fusion.3 = (bf16[16,272,256]{2,1,0:T(8,128)(2,1)}, bf16[16,272,256]{2,1,0:T(8,128)(2,1)S(1)}, bf16[16,272,256]{2,1,0:T(8,128)(2,1)}) fusion(f32[16,272,256]{2,1,0:T(8,128)} %fusion.67, f32[16,272,256]{2,1,0:T(8,128)} %fusion.68, bf16[2048,16,256]{2,0,1:T(8,128)(2,1)} %all-gather.26.cloned.1.call-done, f32[16,272,2048]{2,1,0:T(8,128)} %bitcast.142, ...), kind=kOutput, calls=%fused_computation.24 | convolution fusion | flops 4599054336 | bytes 68043776 | tf_op jit(solution)/shard_map/ecd,def->ecf/dot_general | solution.py:183
  1067.6 25.4 fusion.69
  1093.0 31.1 %convolution_add_fusion = f32[16,272,2048]{2,1,0:T(8,128)} fusion(f32[16,272,2048]{2,1,0:T(8,128)} %fusion.69, bf16[16,272,256]{2,1,0:T(8,128)(2,1)} %get-tuple-element.104, bf16[2048,16,256]{2,0,1:T(8,128)(2,1)} %all-gather.24.cloned.1.call-done), kind=kOutput, calls=%fused_computation.12 | convolution fusion | flops 4572315648 | bytes 90308608 | tf_op jit(solution)/shard_map/ecf,def->ecd/dot_general | solution.py:191
  1124.1 60.5 %scatter_custom_fusion.2 = f32[513,2048]{1,0:T(8,128)} fusion(s32[4352]{0:T(1024)} %copy-done.52, f32[4352,2048]{1,0:T(8,128)} %bitcast.149, f32[]{:T(128)} %constant.32.clone.1), kind=kCustom, calls=%fused_computation.56 | custom fusion | flops 8912896 | bytes 4203008 | tf_op jit(solution)/shard_map/scatter-add | solution.py:195
  1188.8 31.0 %multiply_reduce_fusion = (bf16[16,272]{1,0:T(8,128)(2,1)S(1)}, f32[16,272,2048]{2,1,0:T(8,128)}) fusion(f32[16,272,2048]{2,1,0:T(8,128)} %bitcast.143, bf16[16,272,256]{2,1,0:T(8,128)(2,1)S(1)} %copy-done.16, bf16[2048,16,256]{2,0,1:T(8,128)(2,1)} %all-gather.26.cloned.1.call-done), kind=kOutput, calls=%fused_computation.10 | convolution fusion | flops 4581224448 | bytes 90317312 | tf_op jit(solution)/shard_map/ecf,def->ecd/dot_general | solution.py:168
  1219.8 26.7 bitcast_multiply_fusion
  1246.7 25.6 gather_fusion.3
  1272.5 12.4 psum.103
  1285.0 22.1 scatter_custom_fusion.3
  1307.2 60.9 %scatter_custom_fusion.1 = f32[513,2048]{1,0:T(8,128)} fusion(s32[4352]{0:T(1024)} %copy-done.52, f32[4352,2048]{1,0:T(8,128)} %bitcast_multiply_fusion, f32[]{:T(128)} %constant.32.clone.1), kind=kCustom, calls=%fused_computation.58 | custom fusion | flops 8912896 | bytes 4203008 | tf_op jit(solution)/shard_map/scatter-add | solution.py:174
  1390.6 5.8 all-reduce.6
  1414.9 4.8 convolution_convert_fusion
  1420.0 20.4 convert_bitcast_fusion
  1440.5 18.9 convert_bitcast_fusion.2
  1459.7 19.0 convert_bitcast_fusion.1
  1482.9 44.9 %all-reduce.21.cloned.1.call-done = (bf16[512,2048]{1,0:T(8,128)(2,1)}, bf16[512,2048]{1,0:T(8,128)(2,1)}) async-done(((bf16[512,2048]{1,0:T(8,128)(2,1)}, bf16[512,2048]{1,0:T(8,128)(2,1)}), (bf16[512,2048]{1,0:T(8,128)(2,1)}, bf16[512,2048]{1,0:T(8,128)(2,1)})) %all-reduce.21.cloned.1.call-update) | async-done | bytes 4194320 | tf_op jit(solution)/shard_map/psum | solution.py:200
  1527.7 5.2 fusion.5
  1533.1 21.6 all-reduce.8
  1562.4 36.9 %reduce-scatter.12.cloned.1.call-done = bf16[256,512]{1,0:T(8,128)(2,1)} async-done(((bf16[2048,512]{1,0:T(8,128)(2,1)}), bf16[256,512]{1,0:T(8,128)(2,1)}) %reduce-scatter.12.cloned.1.call-update) | async-done | bytes 262160 | tf_op jit(solution)/shard_map/reduce_scatter | solution.py:313
  1601.1 68.6 %reduce-scatter.10.cloned.1.call-done = bf16[256,512]{1,0:T(8,128)(2,1)} async-done(((bf16[2048,512]{1,0:T(8,128)(2,1)}), bf16[256,512]{1,0:T(8,128)(2,1)}) %reduce-scatter.10.cloned.1.call-update) | async-done | bytes 262160 | tf_op jit(solution)/shard_map/reduce_scatter | solution.py:310
  1671.5 68.8 %reduce-scatter.8.cloned.1.call-done = bf16[256,512]{1,0:T(8,128)(2,1)} async-done(((bf16[2048,512]{1,0:T(8,128)(2,1)}), bf16[256,512]{1,0:T(8,128)(2,1)}) %reduce-scatter.8.cloned.1.call-update) | async-done | bytes 262160 | tf_op jit(solution)/shard_map/reduce_scatter | solution.py:307
  1742.1 68.6 %reduce-scatter.14.cloned.1.call-done = bf16[256,512]{1,0:T(8,128)(2,1)} async-done(((bf16[2048,512]{1,0:T(8,128)(2,1)}), bf16[256,512]{1,0:T(8,128)(2,1)}) %reduce-scatter.14.cloned.1.call-update) | async-done | bytes 262160 | tf_op jit(solution)/shard_map/reduce_scatter | solution.py:316
  1812.5 284.1 %reduce-scatter.20.cloned.1.call-done = bf16[256,16,256]{0,2,1:T(8,128)(2,1)} async-done(((bf16[2048,16,256]{0,2,1:T(8,128)(2,1)}), bf16[256,16,256]{0,2,1:T(8,128)(2,1)}) %reduce-scatter.20.cloned.1.call-update) | async-done | bytes 2097168 | tf_op jit(solution)/shard_map/reduce_scatter | solution.py:325
  2096.5 4.8 copy.137
  2101.3 280.9 %reduce-scatter.16.cloned.1.call-done = bf16[256,16,256]{0,2,1:T(8,128)(2,1)} async-done(((bf16[2048,16,256]{0,2,1:T(8,128)(2,1)}), bf16[256,16,256]{0,2,1:T(8,128)(2,1)}) %reduce-scatter.16.cloned.1.call-update) | async-done | bytes 2097168 | tf_op jit(solution)/shard_map/reduce_scatter | solution.py:319
  2382.2 4.8 copy.135
  2387.0 281.0 %reduce-scatter.18.cloned.1.call-done = bf16[256,16,256]{0,2,1:T(8,128)(2,1)} async-done(((bf16[2048,16,256]{0,2,1:T(8,128)(2,1)}), bf16[256,16,256]{0,2,1:T(8,128)(2,1)}) %reduce-scatter.18.cloned.1.call-update) | async-done | bytes 2097168 | tf_op jit(solution)/shard_map/reduce_scatter | solution.py:322
  2668.0 4.8 copy.136
  (328 shorter events, 130.6 us)
Async XLA Ops:
  7.2 343.0 %copy-start = (bf16[2048,16]{0,1:T(8,128)(2,1)S(1)}, bf16[2048,16]{0,1:T(8,128)(2,1)}, u32[]{:S(2)}) copy-start(bf16[2048,16]{0,1:T(8,128)(2,1)} %param.28) | copy-start | bytes 196612
  7.2 27.7 %all-gather.12.cloned.1.call-start = ((), (), s32[]{:S(2)}) async-start(), calls=%async_computation.7 | async-start | bytes 2621440 | tf_op jit(solution)/shard_map/all_gather | solution.py:73
  7.9 78.4 %all-gather.16.cloned.1.call-start = ((), (), s32[]{:S(2)}) async-start(), calls=%async_computation.9 | async-start | bytes 2359296 | tf_op jit(solution)/shard_map/all_gather | solution.py:88
  8.7 127.6 %all-gather.18.cloned.1.call-start = ((), (), s32[]{:S(2)}) async-start(), calls=%async_computation.10 | async-start | bytes 2359296 | tf_op jit(solution)/shard_map/all_gather | solution.py:89
  9.4 176.7 %all-gather.14.cloned.1.call-start = ((), (), s32[]{:S(2)}) async-start(), calls=%async_computation.8 | async-start | bytes 2359296 | tf_op jit(solution)/shard_map/all_gather | solution.py:90
  10.0 225.9 %all-gather.20.cloned.1.call-start = ((), (), s32[]{:S(2)}) async-start(), calls=%async_computation.11 | async-start | bytes 2359296 | tf_op jit(solution)/shard_map/all_gather | solution.py:138
  10.6 272.3 %all-gather.28.cloned.1.call-start = ((), (), s32[]{:S(2)}) async-start(), calls=%async_computation.16 | async-start | bytes 2621440 | tf_op jit(solution)/shard_map/all_gather | solution.py:74
  11.2 335.8 %all-reduce.15.cloned.1.call-start = ((), (), s32[]{:S(2)}) async-start(), calls=%async_computation.12 | async-start | bytes 8388608 | tf_op jit(solution)/shard_map/psum | solution.py:140
  18.0 168.1 %copy-start.65 = (f32[4,1,512]{2,1,0:T(1,128)}, f32[4,1,512]{2,1,0:T(1,128)S(1)}, u32[]{:S(2)}) copy-start(f32[4,1,512]{2,1,0:T(1,128)S(1)} %convert_element_type.261) | copy-start | bytes 24580
  18.7 127.8 %copy-start.57 = (f32[512]{0:T(512)}, f32[512]{0:T(512)S(1)}, u32[]{:S(2)}) copy-start(f32[512]{0:T(512)S(1)} %convert_element_type.200) | copy-start | bytes 6148
  19.4 127.4 %copy-start.59 = (f32[512]{0:T(512)}, f32[512]{0:T(512)S(1)}, u32[]{:S(2)}) copy-start(f32[512]{0:T(512)S(1)} %convert_element_type.202) | copy-start | bytes 6148
  37.0 53.1 %copy-start.69 = (f32[512]{0:T(512)}, f32[512]{0:T(512)S(1)}, u32[]{:S(2)}) copy-start(f32[512]{0:T(512)S(1)} %multiply_reduce_fusion.6) | copy-start | bytes 6148
  37.0 149.1 %copy-start.71 = (f32[512]{0:T(512)}, f32[512]{0:T(512)S(1)}, u32[]{:S(2)}) copy-start(f32[512]{0:T(512)S(1)} %fusion.58) | copy-start | bytes 6148
  86.4 49.9 %copy-start.9 = (bf16[512,2048]{1,0:T(8,128)(2,1)S(1)}, bf16[512,2048]{1,0:T(8,128)(2,1)}, u32[]{:S(2)}) copy-start(bf16[512,2048]{1,0:T(8,128)(2,1)} %all-gather.12.cloned.1.call-done) | copy-start | bytes 6291460
  90.1 56.3 %copy-start.12 = (f32[512,512]{0,1:T(8,128)}, f32[512,512]{0,1:T(8,128)S(1)}, u32[]{:S(2)}) copy-start(f32[512,512]{0,1:T(8,128)S(1)} %get-tuple-element.136) | copy-start | bytes 3145732
  191.0 49.8 %copy-start.23 = (bf16[4,128,512]{2,1,0:T(8,128)(2,1)}, bf16[4,128,512]{2,1,0:T(8,128)(2,1)S(1)}, u32[]{:S(2)}) copy-start(bf16[4,128,512]{2,1,0:T(8,128)(2,1)S(1)} %fusion.20) | copy-start | bytes 1572868
  240.8 336.3 %all-gather.22.cloned.1.call-start = ((), (), s32[]{:S(2)}) async-start(), calls=%async_computation.13 | async-start | bytes 18874368 | tf_op jit(solution)/shard_map/all_gather | solution.py:158
  244.7 560.6 %all-gather.24.cloned.1.call-start = ((), (), s32[]{:S(2)}) async-start(), calls=%async_computation.14 | async-start | bytes 18874368 | tf_op jit(solution)/shard_map/all_gather | solution.py:159
  248.6 784.8 %all-gather.26.cloned.1.call-start = ((), (), s32[]{:S(2)}) async-start(), calls=%async_computation.15 | async-start | bytes 18874368 | tf_op jit(solution)/shard_map/all_gather | solution.py:167
  252.4 12.6 copy-start.80
  252.4 12.6 copy-start.79
  252.4 1121.1 %all-reduce.17.cloned.1.call-start = ((), (), s32[]{:S(2)}) async-start(), calls=%async_computation.17 | async-start | bytes 4194304 | tf_op jit(solution)/shard_map/psum | solution.py:199
  258.1 91.7 %copy-start.47 = (f32[4,1,512]{2,1,0:T(1,128)}, f32[4,1,512]{2,1,0:T(1,128)S(1)}, u32[]{:S(2)}) copy-start(f32[4,1,512]{2,1,0:T(1,128)S(1)} %convert_element_type.262) | copy-start | bytes 24580
  281.6 39.8 %copy-start.52 = (s32[4352]{0:T(1024)}, s32[4352]{0:T(1024)S(1)}, u32[]{:S(2)}) copy-start(s32[4352]{0:T(1024)S(1)} %get-tuple-element.127) | copy-start | bytes 52228
  352.5 76.2 %copy-start.55 = (f32[512]{0:T(512)}, f32[512]{0:T(512)S(1)}, u32[]{:S(2)}) copy-start(f32[512]{0:T(512)S(1)} %fusion.50) | copy-start | bytes 6148
  352.5 33.3 %copy-start.43 = (s32[512,8]{0,1:T(8,128)S(1)}, s32[512,8]{0,1:T(8,128)}, u32[]{:S(2)}) copy-start(s32[512,8]{0,1:T(8,128)} %param.19) | copy-start | bytes 49156
  352.5 33.6 %copy-start.51 = (s32[5120]{0:T(1024)S(1)}, s32[5120]{0:T(1024)}, u32[]{:S(2)}) copy-start(s32[5120]{0:T(1024)} %pad_clamp_fusion.1) | copy-start | bytes 61444
  409.7 623.8 %copy-start.49 = (f32[16,272]{1,0:T(8,128)}, f32[16,272]{1,0:T(8,128)S(1)}, u32[]{:S(2)}) copy-start(f32[16,272]{1,0:T(8,128)S(1)} %mul.486) | copy-start | bytes 52228
  1067.6 25.4 copy-start.11
  1188.7 292.6 %all-reduce.19.cloned.1.call-start = ((), (), s32[]{:S(2)}) async-start(), calls=%async_computation.22 | async-start | bytes 131072 | tf_op jit(solution)/shard_map/psum | solution.py:286
  1188.8 31.0 %copy-start.45 = (f32[4352]{0:T(1024)S(1)}, f32[4352]{0:T(1024)}, u32[]{:S(2)}) copy-start(f32[4352]{0:T(1024)} %copy-done.44) | copy-start | bytes 52228
  1219.8 26.9 %copy-start.18 = (s32[4096]{0:T(1024)S(1)}, s32[4096]{0:T(1024)}, u32[]{:S(2)}) copy-start(s32[4096]{0:T(1024)} %broadcast_clamp_fusion) | copy-start | bytes 49156
  1246.7 60.5 %copy-start.39 = (f32[512,16]{0,1:T(8,128)S(1)}, f32[512,16]{0,1:T(8,128)}, u32[]{:S(2)}) copy-start(f32[512,16]{0,1:T(8,128)} %copy-done.38) | copy-start | bytes 98308
  1246.7 60.5 %copy-start.54 = (f32[512]{0:T(512)S(1)}, f32[512]{0:T(512)}, u32[]{:S(2)}) copy-start(f32[512]{0:T(512)} %copy-done.53) | copy-start | bytes 6148
  1246.7 60.5 %copy-start.77 = (f32[512]{0:T(512)S(1)}, f32[512]{0:T(512)}, u32[]{:S(2)}) copy-start(f32[512]{0:T(512)} %multiply_divide_fusion) | copy-start | bytes 6148
  1307.2 64.8 %copy-start.56 = (f32[512]{0:T(512)S(1)}, f32[512]{0:T(512)}, u32[]{:S(2)}) copy-start(f32[512]{0:T(512)} %copy-done.55) | copy-start | bytes 6148
  1307.2 64.8 %copy-start.8 = (bf16[512,2048]{1,0:T(8,128)(2,1)S(1)}, bf16[512,2048]{1,0:T(8,128)(2,1)}, u32[]{:S(2)}) copy-start(bf16[512,2048]{1,0:T(8,128)(2,1)} %copy-done.7) | copy-start | bytes 6291460
  1373.1 154.7 %all-reduce.21.cloned.1.call-start = ((), (), s32[]{:S(2)}) async-start(), calls=%async_computation.26 | async-start | bytes 8388608 | tf_op jit(solution)/shard_map/psum | solution.py:200
  1388.8 7.6 copy-start.76
  1389.4 8.8 copy-start.75
  1404.6 194.7 %reduce-scatter.12.cloned.1.call-start = ((), (), s32[]{:S(2)}) async-start(), calls=%async_computation.20 | async-start | bytes 2359296 | tf_op jit(solution)/shard_map/reduce_scatter | solution.py:313
  1409.0 260.7 %reduce-scatter.10.cloned.1.call-start = ((), (), s32[]{:S(2)}) async-start(), calls=%async_computation.19 | async-start | bytes 2359296 | tf_op jit(solution)/shard_map/reduce_scatter | solution.py:310
  1411.9 328.3 %reduce-scatter.8.cloned.1.call-start = ((), (), s32[]{:S(2)}) async-start(), calls=%async_computation.18 | async-start | bytes 2359296 | tf_op jit(solution)/shard_map/reduce_scatter | solution.py:307
  1414.9 395.8 %reduce-scatter.14.cloned.1.call-start = ((), (), s32[]{:S(2)}) async-start(), calls=%async_computation.21 | async-start | bytes 2359296 | tf_op jit(solution)/shard_map/reduce_scatter | solution.py:316
  1419.7 676.8 %reduce-scatter.20.cloned.1.call-start = ((), (), s32[]{:S(2)}) async-start(), calls=%async_computation.25 | async-start | bytes 18874368 | tf_op jit(solution)/shard_map/reduce_scatter | solution.py:325
  1440.5 941.7 %reduce-scatter.16.cloned.1.call-start = ((), (), s32[]{:S(2)}) async-start(), calls=%async_computation.23 | async-start | bytes 18874368 | tf_op jit(solution)/shard_map/reduce_scatter | solution.py:319
  1459.4 1208.6 %reduce-scatter.18.cloned.1.call-start = ((), (), s32[]{:S(2)}) async-start(), calls=%async_computation.24 | async-start | bytes 18874368 | tf_op jit(solution)/shard_map/reduce_scatter | solution.py:322
  1527.7 31.6 %copy-start.70 = (f32[512]{0:T(512)S(1)}, f32[512]{0:T(512)}, u32[]{:S(2)}) copy-start(f32[512]{0:T(512)} %copy-done.69) | copy-start | bytes 6148
  (53 other events, 125.4 us)
Sparse Core Ops, SparseCore 0:
  9.6 25.2 all-gather.11
  37.0 49.2 all-gather.15
  88.5 47.7 all-gather.17
  138.3 47.7 all-gather.13
  188.1 47.7 all-gather.19
  237.3 21.0 all-gather.27
  261.4 85.5 all-reduce.14
  349.3 227.7 all-gather.21
  579.5 225.7 all-gather.23
  807.6 225.7 all-gather.25
  1188.8 49.5 all-reduce.16
  1373.2 66.4 all-reduce.18
  1442.1 85.6 all-reduce.20
  1531.5 67.7 reduce-scatter.11
  1603.1 66.5 reduce-scatter.9
  1673.5 66.7 reduce-scatter.7
  1744.1 66.5 reduce-scatter.13
  1814.8 281.7 reduce-scatter.19
  2100.3 281.8 reduce-scatter.15
  2386.3 281.6 reduce-scatter.17
where the time goes:
time: 2690 us; the launch traced here: 2680 us
  waiting for transfers between devices  1920 us (71%)
  matrix products  261 us (10%)
  other arithmetic  221 us (8%)
  local copies, waits for them, and re-layouts  205 us (8%)
  blocking collectives  56.7 us (2%)
    reduce_scatter x1, waiting for transfers between devices, per_device(): lax.psum_scatter(down_term.astype(jnp.bfloat16), 'wide', scatter_dimensio...  284 us
    reduce_scatter x1, waiting for transfers between devices, per_device(): lax.psum_scatter(up_term.astype(jnp.bfloat16), 'wide', scatter_dimension=...  281 us
    reduce_scatter x1, waiting for transfers between devices, per_device(): lax.psum_scatter(gate_term.astype(jnp.bfloat16), 'wide', scatter_dimensio...  281 us
    all_gather x1, waiting for transfers between devices, per_device(): lax.all_gather(w_up, 'wide', axis=0, tiled=True)  212 us
    all_gather x1, waiting for transfers between devices, per_device(): down_full = lax.all_gather(w_down, 'wide', axis=0, tiled=True)  211 us
    all_gather x1, waiting for transfers between devices, per_device(): lax.all_gather(w_gate, 'wide', axis=0, tiled=True)  148 us
    reduce_scatter x1, waiting for transfers between devices, per_device(): lax.psum_scatter(query_term.astype(jnp.bfloat16), 'wide', scatter_dimensi...  68.8 us
    reduce_scatter x1, waiting for transfers between devices, per_device(): lax.psum_scatter(key_term.astype(jnp.bfloat16), 'wide', scatter_dimension...  68.6 us
  transfers between devices with their start and end apart: 20, of which 17 were waited for; matrix products, arithmetic and copies ran while one was open for 19% of the time, Pallas kernels for 0%

commit v1 on v0

--- a/solution.py
+++ b/solution.py
@@ -164,7 +164,15 @@
     up_pre = jnp.einsum("ecd,def->ecf", expert_rows, up_full, preferred_element_type=jnp.float32)
     hidden_float, swiglu_pull = jax.vjp(swiglu, gate_pre, up_pre)
     hidden_bf = hidden_float.astype(jnp.bfloat16)
-    down_full = lax.all_gather(w_down, "wide", axis=0, tiled=True)
+    ways, here, lap = (lax.axis_size("wide"), lax.axis_index("wide"), w_down.shape[0])
+    line, have = (w_down, 1)
+    while have < ways:
+        line = jnp.concatenate(
+            [line, lax.ppermute(line, "wide", [(d, (d - have) % ways) for d in range(ways)])],
+            axis=0,
+        )
+        have = 2 * have
+    down_full = jnp.roll(line, here * lap, axis=0)
     expert_out = jnp.einsum(
         "ecf,def->ecd", hidden_bf, down_full, preferred_element_type=jnp.float32
     ).reshape(EXPERTS * CAP, model_width)

time: 2690 us -> 2820 us (1.048)
  waiting for transfers between devices: 1920 us -> 2030 us
    ppermute x0 -> x3, waiting for transfers between devices: none -> 689 us  [per_device(): lax.ppermute(line, 'wide', [(d, (d - have) % ways) for d in range(ways)])]
    all_gather x1 -> x0, waiting for transfers between devices: 211 us -> none  [per_device(): down_full = lax.all_gather(w_down, 'wide', axis=0, tiled=True)]
    all_gather x1, waiting for transfers between devices: 212 us -> 8.53 us  [per_device(): lax.all_gather(w_up, 'wide', axis=0, tiled=True)]
    all_gather x1, waiting for transfers between devices: 148 us -> 0.01 us  [per_device(): lax.all_gather(w_gate, 'wide', axis=0, tiled=True)]
    unnamed x173 -> x187, local copies, waits for them, and re-layouts: 39.2 us -> 60.4 us
  transfers between devices with their start and end apart: 20 -> 22, of which waited for: 17 -> 17; matrix products, arithmetic and copies ran while one was open for 19% -> 19% of each run, Pallas kernels for 0% -> 0%
where the time goes in v1:
time: 2820 us; the launch traced here: 2810 us
  waiting for transfers between devices  2030 us (72%)
  matrix products  240 us (9%)
  local copies, waits for them, and re-layouts  233 us (8%)
  other arithmetic  226 us (8%)
  blocking collectives  57.6 us (2%)
    ppermute x3, waiting for transfers between devices, per_device(): lax.ppermute(line, 'wide', [(d, (d - have) % ways) for d in range(ways)])  689 us
    reduce_scatter x1, waiting for transfers between devices, per_device(): lax.psum_scatter(down_term.astype(jnp.bfloat16), 'wide', scatter_dimensio...  284 us
    reduce_scatter x1, waiting for transfers between devices, per_device(): lax.psum_scatter(up_term.astype(jnp.bfloat16), 'wide', scatter_dimension=...  281 us
    reduce_scatter x1, waiting for transfers between devices, per_device(): lax.psum_scatter(gate_term.astype(jnp.bfloat16), 'wide', scatter_dimensio...  281 us
    reduce_scatter x1, waiting for transfers between devices, per_device(): lax.psum_scatter(query_term.astype(jnp.bfloat16), 'wide', scatter_dimensi...  68.8 us
    reduce_scatter x1, waiting for transfers between devices, per_device(): lax.psum_scatter(out_term.astype(jnp.bfloat16), 'wide', scatter_dimension...  68.7 us
    reduce_scatter x1, waiting for transfers between devices, per_device(): lax.psum_scatter(key_term.astype(jnp.bfloat16), 'wide', scatter_dimension...  68.6 us
    scatter-add x1, other arithmetic, per_device(): moe_partial = jnp.zeros((length + 1, model_width), jnp.float32).at[slot_t...  60.9 us
  transfers between devices with their start and end apart: 22, of which 17 were waited for; matrix products, arithmetic and copies ran while one was open for 19% of the time, Pallas kernels for 0%

profile of v1, /device:TPU:0, one launch (start us, length us, event | category | flops | bytes accessed | tf_op | source)
XLA Modules:
  0.0 2808.8 jit_solution(3978545217644959428)
XLA Ops:
  11.9 6.1 all-gather
  22.9 12.0 all-gather.11.cloned.1.call-done
  37.0 49.3 %all-gather.15.cloned.1.call-done = bf16[2048,512]{1,0:T(8,128)(2,1)} async-done(((bf16[256,512]{1,0:T(8,128)(2,1)}), bf16[2048,512]{1,0:T(8,128)(2,1)}) %all-gather.15.cloned.1.call-update) | async-done | bytes 2097168 | tf_op jit(solution)/shard_map/all_gather | solution.py:88
  90.1 46.2 %all-gather.17.cloned.1.call-done = bf16[2048,512]{1,0:T(8,128)(2,1)} async-done(((bf16[256,512]{1,0:T(8,128)(2,1)}), bf16[2048,512]{1,0:T(8,128)(2,1)}) %all-gather.17.cloned.1.call-update) | async-done | bytes 2097168 | tf_op jit(solution)/shard_map/all_gather | solution.py:89
  140.2 5.6 all-reduce.7
  152.6 33.5 %all-gather.13.cloned.1.call-done = bf16[2048,512]{1,0:T(8,128)(2,1)} async-done(((bf16[256,512]{1,0:T(8,128)(2,1)}), bf16[2048,512]{1,0:T(8,128)(2,1)}) %all-gather.13.cloned.1.call-update) | async-done | bytes 2097168 | tf_op jit(solution)/shard_map/all_gather | solution.py:90
  191.0 44.9 %all-gather.19.cloned.1.call-done = bf16[2048,512]{1,0:T(8,128)(2,1)} async-done(((bf16[256,512]{1,0:T(8,128)(2,1)}), bf16[2048,512]{1,0:T(8,128)(2,1)}) %all-gather.19.cloned.1.call-update) | async-done | bytes 2097168 | tf_op jit(solution)/shard_map/all_gather | solution.py:138
  235.9 4.9 fusion.72
  254.3 44.8 %collective-permute-done = bf16[256,16,256]{2,0,1:T(8,128)(2,1)S(1)} collective-permute-done((bf16[256,16,256]{2,0,1:T(8,128)(2,1)S(1)}, bf16[256,16,256]{2,0,1:T(8,128)(2,1)S(1)}, u32[]{:S(2)}, u32[]{:S(2)}) %collective-permute-start) | collective-permute-done | bytes 2097184 | tf_op jit(solution)/shard_map/ppermute | solution.py:171
  302.3 149.0 %collective-permute-done.1 = bf16[512,16,256]{2,0,1:T(8,128)(2,1)S(1)} collective-permute-done((bf16[512,16,256]{2,0,1:T(8,128)(2,1)S(1)}, bf16[512,16,256]{2,0,1:T(8,128)(2,1)S(1)}, u32[]{:S(2)}, u32[]{:S(2)}) %collective-permute-start.1) | collective-permute-done | bytes 4194336 | tf_op jit(solution)/shard_map/ppermute | solution.py:171
  458.5 5.2 all-gather.1
  471.6 15.5 scatter_custom_fusion
  495.6 34.4 %gather_fusion.2 = f32[4352,2048]{1,0:T(8,128)} fusion(f32[513,2048]{1,0:T(8,128)} %concatenate.51, s32[5120]{0:T(1024)S(1)} %pad_clamp_fusion), kind=kCustom, calls=%fused_computation.2 | custom fusion | bytes 71320576 | tf_op jit(solution)/shard_map/gather | solution.py:156
  536.2 33.0 %gather_fusion.4 = f32[4096]{0:T(1024)S(1)} fusion(f32[512,16]{0,1:T(8,128)S(1)} %fusion.52, s32[4096]{0:T(1024)S(1)} %reshape.331), kind=kCustom, calls=%fused_computation.4 | custom fusion | bytes 65536 | tf_op jit(solution)/shard_map/jvp(jit(take_along_axis))/gather | solution.py:145
  569.8 22.8 gather_fusion
  595.1 17.3 gather_fusion.1
  617.5 495.6 %collective-permute-done.2 = bf16[1024,16,256]{2,0,1:T(8,128)(2,1)} collective-permute-done((bf16[1024,16,256]{2,0,1:T(8,128)(2,1)}, bf16[1024,16,256]{2,0,1:T(8,128)(2,1)}, u32[]{:S(2)}, u32[]{:S(2)}) %collective-permute-start.2) | collective-permute-done | bytes 8388640 | tf_op jit(solution)/shard_map/ppermute | solution.py:171
  1113.1 7.7 constant_dynamic-update-slice_fusion.4
  1126.5 7.3 constant_dynamic-update-slice_fusion
  1133.8 15.1 fusion.73
  1149.0 8.5 all-gather.23.cloned.1.call-done
  1157.5 15.1 fusion.74
  1172.6 22.4 multiply_convert_fusion.3
  1195.1 18.9 fusion.75
  1213.9 31.1 %convolution_add_fusion = f32[16,272,2048]{2,1,0:T(8,128)} fusion(f32[16,272,2048]{2,1,0:T(8,128)} %fusion.75, bf16[16,272,256]{2,1,0:T(8,128)(2,1)} %get-tuple-element.104, bf16[2048,16,256]{2,0,1:T(8,128)(2,1)} %all-gather.23.cloned.1.call-done), kind=kOutput, calls=%fused_computation.12 | convolution fusion | flops 4572315648 | bytes 90308608 | tf_op jit(solution)/shard_map/ecf,def->ecd/dot_general | solution.py:199
  1245.1 60.8 %scatter_custom_fusion.2 = f32[513,2048]{1,0:T(8,128)} fusion(s32[4352]{0:T(1024)} %copy-done.56, f32[4352,2048]{1,0:T(8,128)} %bitcast.147, f32[]{:T(128)} %constant.57.clone.1), kind=kCustom, calls=%fused_computation.61 | custom fusion | flops 8912896 | bytes 4203008 | tf_op jit(solution)/shard_map/scatter-add | solution.py:203
  1309.7 30.9 %multiply_reduce_fusion = (bf16[16,272]{1,0:T(8,128)(2,1)S(1)}, f32[16,272,2048]{2,1,0:T(8,128)}) fusion(f32[16,272,2048]{2,1,0:T(8,128)} %bitcast.141, bf16[16,272,256]{2,1,0:T(8,128)(2,1)S(1)} %get-tuple-element.106, bf16[4096,16,256]{2,0,1:T(8,128)(2,1)} %constant_dynamic-update-slice_fusion, s32[]{:T(128)S(6)} %select_n.72), kind=kOutput, calls=%fused_computation.10 | convolution fusion | flops 4581224448 | bytes 90317312 | tf_op jit(solution)/shard_map/ecf,def->ecd/dot_general | solution.py:176
  1340.6 26.8 bitcast_multiply_fusion
  1367.6 25.6 gather_fusion.3
  1393.4 12.8 psum.103
  1406.3 22.1 scatter_custom_fusion.3
  1428.5 60.9 %scatter_custom_fusion.1 = f32[513,2048]{1,0:T(8,128)} fusion(s32[4352]{0:T(1024)} %copy-done.56, f32[4352,2048]{1,0:T(8,128)} %bitcast_multiply_fusion, f32[]{:T(128)} %constant.57.clone.1), kind=kCustom, calls=%fused_computation.63 | custom fusion | flops 8912896 | bytes 4203008 | tf_op jit(solution)/shard_map/scatter-add | solution.py:182
  1511.9 6.3 all-reduce.6
  1536.8 4.9 convolution_convert_fusion
  1542.0 20.5 convert_bitcast_fusion
  1562.6 18.8 convert_bitcast_fusion.2
  1581.8 19.0 convert_bitcast_fusion.1
  1604.9 50.9 %all-reduce.21.cloned.1.call-done = (bf16[512,2048]{1,0:T(8,128)(2,1)}, bf16[512,2048]{1,0:T(8,128)(2,1)}) async-done(((bf16[512,2048]{1,0:T(8,128)(2,1)}, bf16[512,2048]{1,0:T(8,128)(2,1)}), (bf16[512,2048]{1,0:T(8,128)(2,1)}, bf16[512,2048]{1,0:T(8,128)(2,1)})) %all-reduce.21.cloned.1.call-update) | async-done | bytes 4194320 | tf_op jit(solution)/shard_map/psum | solution.py:208
  1655.8 5.3 fusion.8
  1661.1 21.7 all-reduce.8
  1690.6 37.3 %reduce-scatter.12.cloned.1.call-done = bf16[256,512]{1,0:T(8,128)(2,1)} async-done(((bf16[2048,512]{1,0:T(8,128)(2,1)}), bf16[256,512]{1,0:T(8,128)(2,1)}) %reduce-scatter.12.cloned.1.call-update) | async-done | bytes 262160 | tf_op jit(solution)/shard_map/reduce_scatter | solution.py:321
  1729.7 68.6 %reduce-scatter.10.cloned.1.call-done = bf16[256,512]{1,0:T(8,128)(2,1)} async-done(((bf16[2048,512]{1,0:T(8,128)(2,1)}), bf16[256,512]{1,0:T(8,128)(2,1)}) %reduce-scatter.10.cloned.1.call-update) | async-done | bytes 262160 | tf_op jit(solution)/shard_map/reduce_scatter | solution.py:318
  1800.1 68.8 %reduce-scatter.8.cloned.1.call-done = bf16[256,512]{1,0:T(8,128)(2,1)} async-done(((bf16[2048,512]{1,0:T(8,128)(2,1)}), bf16[256,512]{1,0:T(8,128)(2,1)}) %reduce-scatter.8.cloned.1.call-update) | async-done | bytes 262160 | tf_op jit(solution)/shard_map/reduce_scatter | solution.py:315
  1870.6 68.7 %reduce-scatter.14.cloned.1.call-done = bf16[256,512]{1,0:T(8,128)(2,1)} async-done(((bf16[2048,512]{1,0:T(8,128)(2,1)}), bf16[256,512]{1,0:T(8,128)(2,1)}) %reduce-scatter.14.cloned.1.call-update) | async-done | bytes 262160 | tf_op jit(solution)/shard_map/reduce_scatter | solution.py:324
  1941.2 284.1 %reduce-scatter.20.cloned.1.call-done = bf16[256,16,256]{0,2,1:T(8,128)(2,1)} async-done(((bf16[2048,16,256]{0,2,1:T(8,128)(2,1)}), bf16[256,16,256]{0,2,1:T(8,128)(2,1)}) %reduce-scatter.20.cloned.1.call-update) | async-done | bytes 2097168 | tf_op jit(solution)/shard_map/reduce_scatter | solution.py:333
  2225.3 4.8 copy.157
  2230.1 280.8 %reduce-scatter.16.cloned.1.call-done = bf16[256,16,256]{0,2,1:T(8,128)(2,1)} async-done(((bf16[2048,16,256]{0,2,1:T(8,128)(2,1)}), bf16[256,16,256]{0,2,1:T(8,128)(2,1)}) %reduce-scatter.16.cloned.1.call-update) | async-done | bytes 2097168 | tf_op jit(solution)/shard_map/reduce_scatter | solution.py:327
  2515.6 281.4 %reduce-scatter.18.cloned.1.call-done = bf16[256,16,256]{0,2,1:T(8,128)(2,1)} async-done(((bf16[2048,16,256]{0,2,1:T(8,128)(2,1)}), bf16[256,16,256]{0,2,1:T(8,128)(2,1)}) %reduce-scatter.18.cloned.1.call-update) | async-done | bytes 2097168 | tf_op jit(solution)/shard_map/reduce_scatter | solution.py:330
  (348 shorter events, 164.9 us)
Async XLA Ops:
  7.2 526.7 %copy-start = (bf16[2048,16]{0,1:T(8,128)(2,1)S(1)}, bf16[2048,16]{0,1:T(8,128)(2,1)}, u32[]{:S(2)}) copy-start(bf16[2048,16]{0,1:T(8,128)(2,1)} %param.28) | copy-start | bytes 196612
  7.2 27.7 all-gather.11.cloned.1.call-start
  7.9 78.4 %all-gather.15.cloned.1.call-start = ((), (), s32[]{:S(2)}) async-start(), calls=%async_computation.9 | async-start | bytes 2359296 | tf_op jit(solution)/shard_map/all_gather | solution.py:88
  8.7 127.6 %all-gather.17.cloned.1.call-start = ((), (), s32[]{:S(2)}) async-start(), calls=%async_computation.10 | async-start | bytes 2359296 | tf_op jit(solution)/shard_map/all_gather | solution.py:89
  9.4 176.7 %all-gather.13.cloned.1.call-start = ((), (), s32[]{:S(2)}) async-start(), calls=%async_computation.8 | async-start | bytes 2359296 | tf_op jit(solution)/shard_map/all_gather | solution.py:90
  10.0 225.9 %all-gather.19.cloned.1.call-start = ((), (), s32[]{:S(2)}) async-start(), calls=%async_computation.11 | async-start | bytes 2359296 | tf_op jit(solution)/shard_map/all_gather | solution.py:138
  10.6 480.9 %all-gather.25.cloned.1.call-start = ((), (), s32[]{:S(2)}) async-start(), calls=%async_computation.15 | async-start | bytes 2621440 | tf_op jit(solution)/shard_map/all_gather | solution.py:74
  11.2 519.4 %all-reduce.15.cloned.1.call-start = ((), (), s32[]{:S(2)}) async-start(), calls=%async_computation.12 | async-start | bytes 8388608 | tf_op jit(solution)/shard_map/psum | solution.py:140
  18.0 168.1 %copy-start.69 = (f32[4,1,512]{2,1,0:T(1,128)}, f32[4,1,512]{2,1,0:T(1,128)S(1)}, u32[]{:S(2)}) copy-start(f32[4,1,512]{2,1,0:T(1,128)S(1)} %convert_element_type.261) | copy-start | bytes 24580
  18.7 127.8 %copy-start.61 = (f32[512]{0:T(512)}, f32[512]{0:T(512)S(1)}, u32[]{:S(2)}) copy-start(f32[512]{0:T(512)S(1)} %convert_element_type.200) | copy-start | bytes 6148
  19.4 127.4 %copy-start.63 = (f32[512]{0:T(512)}, f32[512]{0:T(512)S(1)}, u32[]{:S(2)}) copy-start(f32[512]{0:T(512)S(1)} %convert_element_type.202) | copy-start | bytes 6148
  37.0 53.1 %copy-start.73 = (f32[512]{0:T(512)}, f32[512]{0:T(512)S(1)}, u32[]{:S(2)}) copy-start(f32[512]{0:T(512)S(1)} %multiply_reduce_fusion.6) | copy-start | bytes 6148
  37.0 149.1 %copy-start.75 = (f32[512]{0:T(512)}, f32[512]{0:T(512)S(1)}, u32[]{:S(2)}) copy-start(f32[512]{0:T(512)S(1)} %fusion.61) | copy-start | bytes 6148
  86.4 49.9 %copy-start.11 = (bf16[512,2048]{1,0:T(8,128)(2,1)S(1)}, bf16[512,2048]{1,0:T(8,128)(2,1)}, u32[]{:S(2)}) copy-start(bf16[512,2048]{1,0:T(8,128)(2,1)} %all-gather.11.cloned.1.call-done) | copy-start | bytes 6291460
  90.1 56.3 %copy-start.16 = (f32[512,512]{0,1:T(8,128)}, f32[512,512]{0,1:T(8,128)S(1)}, u32[]{:S(2)}) copy-start(f32[512,512]{0,1:T(8,128)S(1)} %get-tuple-element.138) | copy-start | bytes 3145732
  191.0 49.8 %copy-start.27 = (bf16[4,128,512]{2,1,0:T(8,128)(2,1)}, bf16[4,128,512]{2,1,0:T(8,128)(2,1)S(1)}, u32[]{:S(2)}) copy-start(bf16[4,128,512]{2,1,0:T(8,128)(2,1)S(1)} %fusion.23) | copy-start | bytes 1572868
  240.8 893.0 %all-gather.21.cloned.1.call-start = ((), (), s32[]{:S(2)}) async-start(), calls=%async_computation.13 | async-start | bytes 18874368 | tf_op jit(solution)/shard_map/all_gather | solution.py:158
  244.6 912.8 %all-gather.23.cloned.1.call-start = ((), (), s32[]{:S(2)}) async-start(), calls=%async_computation.14 | async-start | bytes 18874368 | tf_op jit(solution)/shard_map/all_gather | solution.py:159
  248.7 1246.2 %all-reduce.17.cloned.1.call-start = ((), (), s32[]{:S(2)}) async-start(), calls=%async_computation.16 | async-start | bytes 4194304 | tf_op jit(solution)/shard_map/psum | solution.py:207
  252.6 46.6 %collective-permute-start = (bf16[256,16,256]{2,0,1:T(8,128)(2,1)S(1)}, bf16[256,16,256]{2,0,1:T(8,128)(2,1)S(1)}, u32[]{:S(2)}, u32[]{:S(2)}) collective-permute-start(bf16[256,16,256]{2,0,1:T(8,128)(2,1)S(1)} %get-tuple-element.108), channel_id=1, source_target_pairs={{0,28},{4,0},{8,4},{12,8},{16,12},{20,16},{24,20},{28,24},{1,29},{... | collective-permute-start | bytes 6291464 | tf_op jit(solution)/shard_map/ppermute | solution.py:171
  299.2 156.5 %copy-start.13 = (bf16[256,16,256]{2,0,1:T(8,128)(2,1)}, bf16[256,16,256]{2,0,1:T(8,128)(2,1)S(1)}, u32[]{:S(2)}) copy-start(bf16[256,16,256]{2,0,1:T(8,128)(2,1)S(1)} %collective-permute-done) | copy-start | bytes 6291460
  299.5 158.5 %copy-start.46 = (s32[512,8]{0,1:T(8,128)S(1)}, s32[512,8]{0,1:T(8,128)}, u32[]{:S(2)}) copy-start(s32[512,8]{0,1:T(8,128)} %param.19) | copy-start | bytes 49156
  299.6 158.9 %copy-start.82 = (bf16[512]{0:T(512)(128)(2,1)S(1)}, bf16[512]{0:T(512)(128)(2,1)}, u32[]{:S(2)}) copy-start(bf16[512]{0:T(512)(128)(2,1)} %param.27) | copy-start | bytes 3076
  299.6 151.8 %collective-permute-start.1 = (bf16[512,16,256]{2,0,1:T(8,128)(2,1)S(1)}, bf16[512,16,256]{2,0,1:T(8,128)(2,1)S(1)}, u32[]{:S(2)}, u32[]{:S(2)}) collective-permute-start(bf16[512,16,256]{2,0,1:T(8,128)(2,1)S(1)} %pad_maximum_fusion.1), channel_id=1, source_target_pairs={{0,24},{4,28},{8,0},{12,4},{16,8},{20,12},{24,16},{28,20},{1,25},{... | collective-permute-start | bytes 12582920 | tf_op jit(solution)/shard_map/ppermute | solution.py:171
  455.9 657.2 %collective-permute-start.2 = (bf16[1024,16,256]{2,0,1:T(8,128)(2,1)}, bf16[1024,16,256]{2,0,1:T(8,128)(2,1)}, u32[]{:S(2)}, u32[]{:S(2)}) collective-permute-start(bf16[1024,16,256]{2,0,1:T(8,128)(2,1)} %pad_maximum_fusion), channel_id=1, source_target_pairs={{0,16},{4,20},{8,24},{12,28},{16,0},{20,4},{24,8},{28,12},{1,17},{... | collective-permute-start | bytes 25165832 | tf_op jit(solution)/shard_map/ppermute | solution.py:171
  463.7 69.8 %copy-start.51 = (f32[4,1,512]{2,1,0:T(1,128)}, f32[4,1,512]{2,1,0:T(1,128)S(1)}, u32[]{:S(2)}) copy-start(f32[4,1,512]{2,1,0:T(1,128)S(1)} %convert_element_type.262) | copy-start | bytes 24580
  536.1 76.3 %copy-start.59 = (f32[512]{0:T(512)}, f32[512]{0:T(512)S(1)}, u32[]{:S(2)}) copy-start(f32[512]{0:T(512)S(1)} %fusion.53) | copy-start | bytes 6148
  536.2 33.3 %copy-start.47 = (s32[512,8]{0,1:T(8,128)S(1)}, s32[512,8]{0,1:T(8,128)}, u32[]{:S(2)}) copy-start(s32[512,8]{0,1:T(8,128)} %param.19) | copy-start | bytes 49156
  536.2 33.6 %copy-start.55 = (s32[5120]{0:T(1024)S(1)}, s32[5120]{0:T(1024)}, u32[]{:S(2)}) copy-start(s32[5120]{0:T(1024)} %pad_clamp_fusion.1) | copy-start | bytes 61444
  593.3 579.3 %copy-start.53 = (f32[16,272]{1,0:T(8,128)}, f32[16,272]{1,0:T(8,128)S(1)}, u32[]{:S(2)}) copy-start(f32[16,272]{1,0:T(8,128)S(1)} %mul.490) | copy-start | bytes 52228
  617.5 503.3 %copy-start.20 = (bf16[256,16,256]{2,1,0:T(8,128)(2,1)S(1)}, bf16[256,16,256]{2,1,0:T(8,128)(2,1)}, u32[]{:S(2)}) copy-start(bf16[256,16,256]{2,1,0:T(8,128)(2,1)} %param.31) | copy-start | bytes 6291460
  1195.1 114.6 %copy-start.15 = (bf16[16,272,256]{2,1,0:T(8,128)(2,1)}, bf16[16,272,256]{2,1,0:T(8,128)(2,1)S(1)}, u32[]{:S(2)}) copy-start(bf16[16,272,256]{2,1,0:T(8,128)(2,1)S(1)} %get-tuple-element.106) | copy-start | bytes 6684676
  1309.7 293.7 %all-reduce.19.cloned.1.call-start = ((), (), s32[]{:S(2)}) async-start(), calls=%async_computation.21 | async-start | bytes 131072 | tf_op jit(solution)/shard_map/psum | solution.py:294
  1309.7 30.9 %copy-start.49 = (f32[4352]{0:T(1024)S(1)}, f32[4352]{0:T(1024)}, u32[]{:S(2)}) copy-start(f32[4352]{0:T(1024)} %copy-done.48) | copy-start | bytes 52228
  1367.5 60.9 %copy-start.43 = (f32[512,16]{0,1:T(8,128)S(1)}, f32[512,16]{0,1:T(8,128)}, u32[]{:S(2)}) copy-start(f32[512,16]{0,1:T(8,128)} %copy-done.42) | copy-start | bytes 98308
  1367.5 60.9 %copy-start.58 = (f32[512]{0:T(512)S(1)}, f32[512]{0:T(512)}, u32[]{:S(2)}) copy-start(f32[512]{0:T(512)} %copy-done.57) | copy-start | bytes 6148
  1367.6 60.9 %copy-start.81 = (f32[512]{0:T(512)S(1)}, f32[512]{0:T(512)}, u32[]{:S(2)}) copy-start(f32[512]{0:T(512)} %multiply_divide_fusion) | copy-start | bytes 6148
  1428.5 64.8 %copy-start.60 = (f32[512]{0:T(512)S(1)}, f32[512]{0:T(512)}, u32[]{:S(2)}) copy-start(f32[512]{0:T(512)} %copy-done.59) | copy-start | bytes 6148
  1428.5 64.8 %copy-start.10 = (bf16[512,2048]{1,0:T(8,128)(2,1)S(1)}, bf16[512,2048]{1,0:T(8,128)(2,1)}, u32[]{:S(2)}) copy-start(bf16[512,2048]{1,0:T(8,128)(2,1)} %copy-done.9) | copy-start | bytes 6291460
  1494.4 161.4 %all-reduce.21.cloned.1.call-start = ((), (), s32[]{:S(2)}) async-start(), calls=%async_computation.25 | async-start | bytes 8388608 | tf_op jit(solution)/shard_map/psum | solution.py:208
  1526.4 201.4 %reduce-scatter.12.cloned.1.call-start = ((), (), s32[]{:S(2)}) async-start(), calls=%async_computation.19 | async-start | bytes 2359296 | tf_op jit(solution)/shard_map/reduce_scatter | solution.py:321
  1530.9 267.4 %reduce-scatter.10.cloned.1.call-start = ((), (), s32[]{:S(2)}) async-start(), calls=%async_computation.18 | async-start | bytes 2359296 | tf_op jit(solution)/shard_map/reduce_scatter | solution.py:318
  1533.8 335.0 %reduce-scatter.8.cloned.1.call-start = ((), (), s32[]{:S(2)}) async-start(), calls=%async_computation.17 | async-start | bytes 2359296 | tf_op jit(solution)/shard_map/reduce_scatter | solution.py:315
  1536.8 402.6 %reduce-scatter.14.cloned.1.call-start = ((), (), s32[]{:S(2)}) async-start(), calls=%async_computation.20 | async-start | bytes 2359296 | tf_op jit(solution)/shard_map/reduce_scatter | solution.py:324
  1541.7 683.6 %reduce-scatter.20.cloned.1.call-start = ((), (), s32[]{:S(2)}) async-start(), calls=%async_computation.24 | async-start | bytes 18874368 | tf_op jit(solution)/shard_map/reduce_scatter | solution.py:333
  1562.5 948.3 %reduce-scatter.16.cloned.1.call-start = ((), (), s32[]{:S(2)}) async-start(), calls=%async_computation.22 | async-start | bytes 18874368 | tf_op jit(solution)/shard_map/reduce_scatter | solution.py:327
  1581.5 1215.6 %reduce-scatter.18.cloned.1.call-start = ((), (), s32[]{:S(2)}) async-start(), calls=%async_computation.23 | async-start | bytes 18874368 | tf_op jit(solution)/shard_map/reduce_scatter | solution.py:330
  1655.8 31.7 %copy-start.74 = (f32[512]{0:T(512)S(1)}, f32[512]{0:T(512)}, u32[]{:S(2)}) copy-start(f32[512]{0:T(512)} %copy-done.73) | copy-start | bytes 6148
  (59 other events, 213.3 us)
Sparse Core Ops, SparseCore 0:
  9.6 25.2 all-gather.10
  37.0 49.2 all-gather.14
  88.5 47.7 all-gather.16
  138.3 47.7 all-gather.12
  188.1 47.7 all-gather.18
  237.3 21.0 all-gather.24
  261.3 85.4 all-reduce.14
  349.3 513.8 all-gather.20
  865.6 291.8 all-gather.22
  1309.8 57.4 all-reduce.16
  1494.5 73.3 all-reduce.18
  1570.1 85.6 all-reduce.20
  1659.7 68.0 reduce-scatter.11
  1731.6 66.5 reduce-scatter.9
  1802.1 66.7 reduce-scatter.7
  1872.6 66.7 reduce-scatter.13
  1943.5 281.7 reduce-scatter.19
  2229.0 281.8 reduce-scatter.15
  2515.1 281.8 reduce-scatter.17
